TPU v7x, 32 devices: a whole 2x2x4 slice. The times are simulated.
32 devices in a mesh: blk: 16 (over z, y, core), rep: 2 (over x).
Axes of the slice: x: 2, y: 2, z: 4, core: 2. Of those that a mesh axis runs over, the one named last changes fastest.
Arguments:
- features: bfloat16 [16384, 256], P('blk'), may hold values from -6 to 6
- weight_self: bfloat16 [256, 256], replicated, may hold values from -0.375 to 0.375
- weight_neighbor: bfloat16 [256, 256], replicated, may hold values from -0.375 to 0.375
- bias_vector: float32 [256], replicated, may hold values from -3 to 3
- tile_row: int32 [16, 16, 64], P('blk', 'rep'), may hold values from 0 to 7
- tile_column: int32 [16, 16, 64], P('blk', 'rep'), may hold values from 0 to 7
- tile_value: int32 [16, 16, 64], P('blk', 'rep'), may hold values from 0 to 127
- tile_count: int32 [16, 16], P('blk', 'rep'), may hold values from 16 to 64
- tile_table: bfloat16 [4096, 128, 128], P(('blk', 'rep')), may hold values from -0.0625 to 0.0625
- cotangent: bfloat16 [16384, 256], P('blk'), may hold values from -6 to 6
Outputs:
- activations: bfloat16 [16384, 256], P('blk')
- grad_features: bfloat16 [16384, 256], P('blk')
- grad_weight_self: float32 [256, 256], replicated
- grad_weight_neighbor: float32 [256, 256], replicated
- grad_bias: float32 [256], replicated
All inputs are finite; a program needn't handle non-finite values.
Results may differ from a plain program's by a relative error of at most 0.025.
Values may be sent and summed in bfloat16 or wider, within the bound.
A program may use at most 64 MiB of HBM per device.

v0:
```python
import jax
import jax.numpy as jnp
from jax import lax
from jax.sharding import PartitionSpec as P


def from_behind(array, axis, by):
    length = lax.axis_size(axis)
    return lax.ppermute(array, axis, [(i, (i + by) % length) for i in range(length)])


def gather_terms(tile_table, source_blocks, row_pick, column_pick, value_pick, live_count, forward):
    slot_count = row_pick.shape[0]
    block_count = source_blocks.shape[0]
    is_live = jnp.arange(slot_count) < live_count
    tile_values = jnp.take(tile_table, value_pick, axis=0)
    if forward:
        picked = jnp.take(source_blocks, column_pick, axis=0)
        products = jnp.einsum(
            "kab,kbf->kaf", tile_values, picked, preferred_element_type=jnp.float32
        )
        target_pick = row_pick
    else:
        picked = jnp.take(source_blocks, row_pick, axis=0)
        products = jnp.einsum(
            "kab,kaf->kbf", tile_values, picked, preferred_element_type=jnp.float32
        )
        target_pick = column_pick
    placing = (
        (target_pick[:, None] == jnp.arange(block_count)[None, :]) & is_live[:, None]
    ).astype(jnp.float32)
    return jnp.einsum("kr,kaf->raf", placing, products, preferred_element_type=jnp.float32)


def on_device(
    features,
    weight_self,
    weight_neighbor,
    bias_vector,
    tile_row,
    tile_column,
    tile_value,
    tile_count,
    tile_table,
    cotangent,
):
    cycle_length = lax.axis_size("blk")
    replicas = lax.axis_size("rep")
    step_count = cycle_length // replicas
    rep_bits = replicas.bit_length() - 1
    replica = lax.axis_index("rep")
    row_total, feature_width = features.shape
    tile_size = tile_table.shape[1]
    block_count = row_total // tile_size
    row_lists = tile_row[0]
    column_lists = tile_column[0]
    value_lists = tile_value[0]
    live_counts = tile_count[0]

    def step_term(source_blocks, offset, forward):
        return gather_terms(
            tile_table,
            source_blocks,
            lax.dynamic_index_in_dim(row_lists, offset, 0, False),
            lax.dynamic_index_in_dim(column_lists, offset, 0, False),
            lax.dynamic_index_in_dim(value_lists, offset, 0, False),
            lax.dynamic_index_in_dim(live_counts, offset, 0, False),
            forward,
        )

    def shape_blocks(matrix):
        return matrix.reshape(block_count, tile_size, feature_width)

    feature_panel = features
    for bit_index in range(rep_bits):
        shifted = from_behind(feature_panel, "blk", step_count << bit_index)
        feature_panel = jnp.where(replica // (1 << bit_index) % 2 == 1, shifted, feature_panel)
    partial_sum = step_term(shape_blocks(feature_panel), 0, True)

    def cycle_step(offset, carry):
        panel_now, running = carry
        panel_now = from_behind(panel_now, "blk", 1)
        return (panel_now, running + step_term(shape_blocks(panel_now), offset, True))

    feature_panel, partial_sum = lax.fori_loop(
        1, step_count, cycle_step, (feature_panel, partial_sum)
    )
    partial_sum = partial_sum.reshape(row_total, feature_width)
    aggregate = lax.psum(partial_sum, "rep")
    aggregate_b = aggregate.astype(jnp.bfloat16)
    before = jnp.dot(features, weight_self, preferred_element_type=jnp.float32)
    before = (
        before
        + jnp.dot(aggregate_b, weight_neighbor, preferred_element_type=jnp.float32)
        + bias_vector
    )
    sigmoid_pre = jax.nn.sigmoid(before)
    output_rows = (before * sigmoid_pre).astype(jnp.bfloat16)
    derivative = sigmoid_pre * (1.0 + before * (1.0 - sigmoid_pre))
    grad_pre = (cotangent.astype(jnp.float32) * derivative).astype(jnp.bfloat16)
    contract_rows = (((0,), (0,)), ((), ()))
    contract_columns = (((1,), (1,)), ((), ()))
    grad_self = lax.dot_general(
        features, grad_pre, contract_rows, preferred_element_type=jnp.float32
    )
    grad_neighbor = lax.dot_general(
        aggregate_b, grad_pre, contract_rows, preferred_element_type=jnp.float32
    )
    grad_offset = jnp.sum(grad_pre.astype(jnp.float32), axis=0)
    self_term = lax.dot_general(
        grad_pre, weight_self, contract_columns, preferred_element_type=jnp.float32
    )
    sent_back = lax.dot_general(
        grad_pre, weight_neighbor, contract_columns, preferred_element_type=jnp.float32
    ).astype(jnp.bfloat16)
    grad_self, grad_neighbor, grad_offset = (
        lax.psum(grad_self.astype(jnp.bfloat16), "blk").astype(jnp.float32),
        lax.psum(grad_neighbor.astype(jnp.bfloat16), "blk").astype(jnp.float32),
        lax.psum(grad_offset.astype(jnp.bfloat16), "blk").astype(jnp.float32),
    )
    back_blocks = shape_blocks(sent_back)
    pushed = step_term(back_blocks, step_count - 1, False)

    def push_step(offset, running):
        running = from_behind(running, "blk", -1)
        return running + step_term(back_blocks, step_count - 1 - offset, False)

    pushed = lax.fori_loop(1, step_count, push_step, pushed)
    for bit_index in range(rep_bits):
        shifted = from_behind(
            pushed.astype(jnp.bfloat16), "blk", -(step_count << bit_index)
        ).astype(pushed.dtype)
        pushed = jnp.where(replica // (1 << bit_index) % 2 == 1, shifted, pushed)
    pushed = pushed.reshape(row_total, feature_width)
    neighbor_term = lax.psum(pushed.astype(jnp.bfloat16), "rep").astype(jnp.float32)
    grad_features = (self_term + neighbor_term).astype(jnp.bfloat16)
    return (output_rows, grad_features, grad_self, grad_neighbor, grad_offset)


def solution(mesh):
    placed = (
        P("blk", None),
        P(),
        P(),
        P(),
        P("blk", "rep", None),
        P("blk", "rep", None),
        P("blk", "rep", None),
        P("blk", "rep"),
        P(("blk", "rep"), None, None),
        P("blk", None),
    )
    return jax.shard_map(
        on_device,
        mesh=mesh,
        in_specs=placed,
        out_specs=(P("blk", None), P("blk", None), P(), P(), P()),
        check_vma=False,
    )
```

profile of v0, /device:TPU:0, one launch (start us, length us, event | category | flops | bytes accessed | tf_op | source)
XLA Modules:
  0.0 519.6 jit_solution(10854658101296210277)
XLA Ops:
  7.2 4.1 collective-permute-start.2
  19.4 4.4 gather_fusion.6
  25.8 9.0 %collective-permute-done.2 = bf16[1024,256]{1,0:T(8,128)(2,1)} collective-permute-done((bf16[1024,256]{1,0:T(8,128)(2,1)}, bf16[1024,256]{1,0:T(8,128)(2,1)}, u32[]{:S(2)}, u32[]{:S(2)}) %collective-permute-start.2) | collective-permute-done | bytes 524320 | tf_op jit(solution)/shard_map/ppermute | solution.py:9
  44.6 147.8 %while.32 = (s32[]{:T(128)}, bf16[1024,256]{1,0:T(8,128)(2,1)S(1)}, f32[8,128,256]{2,0,1:T(8,128)}, s32[8,64]{1,0:T(8,128)}, s32[8]{0:T(128)S(1)}, /*index=5*/s3...) while((s32[]{:T(128)}, bf16[1024,256]{1,0:T(8,128)(2,1)S(1)}, ...), condition=%wide.region_1.4_spmd, body=%wide.region_0.3_spmd.sunk | while | flops 573837120 | bytes 40906124 | solution.py:85
  50.4 5.5 %collective-permute-done = bf16[1024,256]{1,0:T(8,128)(2,1)S(1)} collective-permute-done((bf16[1024,256]{1,0:T(8,128)(2,1)S(1)}, bf16[1024,256]{1,0:T(8,128)(2,1)S(1)}, u32[]{:S(2)}, u32[]{:S(2)}) %collective-permute-start) | collective-permute-done | bytes 524320 | tf_op jit(solution)/shard_map/while/body/eval_jaxpr/ppermute | solution.py:9
  71.5 5.5 %collective-permute-done = bf16[1024,256]{1,0:T(8,128)(2,1)S(1)} collective-permute-done((bf16[1024,256]{1,0:T(8,128)(2,1)S(1)}, bf16[1024,256]{1,0:T(8,128)(2,1)S(1)}, u32[]{:S(2)}, u32[]{:S(2)}) %collective-permute-start) | collective-permute-done | bytes 524320 | tf_op jit(solution)/shard_map/while/body/eval_jaxpr/ppermute | solution.py:9
  92.6 5.5 %collective-permute-done = bf16[1024,256]{1,0:T(8,128)(2,1)S(1)} collective-permute-done((bf16[1024,256]{1,0:T(8,128)(2,1)S(1)}, bf16[1024,256]{1,0:T(8,128)(2,1)S(1)}, u32[]{:S(2)}, u32[]{:S(2)}) %collective-permute-start) | collective-permute-done | bytes 524320 | tf_op jit(solution)/shard_map/while/body/eval_jaxpr/ppermute | solution.py:9
  113.7 5.5 %collective-permute-done = bf16[1024,256]{1,0:T(8,128)(2,1)S(1)} collective-permute-done((bf16[1024,256]{1,0:T(8,128)(2,1)S(1)}, bf16[1024,256]{1,0:T(8,128)(2,1)S(1)}, u32[]{:S(2)}, u32[]{:S(2)}) %collective-permute-start) | collective-permute-done | bytes 524320 | tf_op jit(solution)/shard_map/while/body/eval_jaxpr/ppermute | solution.py:9
  134.9 5.5 %collective-permute-done = bf16[1024,256]{1,0:T(8,128)(2,1)S(1)} collective-permute-done((bf16[1024,256]{1,0:T(8,128)(2,1)S(1)}, bf16[1024,256]{1,0:T(8,128)(2,1)S(1)}, u32[]{:S(2)}, u32[]{:S(2)}) %collective-permute-start) | collective-permute-done | bytes 524320 | tf_op jit(solution)/shard_map/while/body/eval_jaxpr/ppermute | solution.py:9
  156.0 5.5 %collective-permute-done = bf16[1024,256]{1,0:T(8,128)(2,1)S(1)} collective-permute-done((bf16[1024,256]{1,0:T(8,128)(2,1)S(1)}, bf16[1024,256]{1,0:T(8,128)(2,1)S(1)}, u32[]{:S(2)}, u32[]{:S(2)}) %collective-permute-start) | collective-permute-done | bytes 524320 | tf_op jit(solution)/shard_map/while/body/eval_jaxpr/ppermute | solution.py:9
  177.1 5.5 %collective-permute-done = bf16[1024,256]{1,0:T(8,128)(2,1)S(1)} collective-permute-done((bf16[1024,256]{1,0:T(8,128)(2,1)S(1)}, bf16[1024,256]{1,0:T(8,128)(2,1)S(1)}, u32[]{:S(2)}, u32[]{:S(2)}) %collective-permute-start) | collective-permute-done | bytes 524320 | tf_op jit(solution)/shard_map/while/body/eval_jaxpr/ppermute | solution.py:9
  194.0 23.9 %all-reduce.8 = bf16[1024,256]{1,0:T(8,128)(2,1)S(1)} all-reduce(f32[1024,256]{1,0:T(8,128)S(1)} %bitcast.97), channel_id=1, replica_groups=mesh['blk'=16,'rep'=2] {'rep'}, use_global_device_ids=true, to_apply=%region_2.5 | all-reduce | flops 262144 | bytes 1572864 | tf_op jit(solution)/shard_map/psum | solution.py:89
  231.6 148.3 %while.33 = (s32[]{:T(128)}, f32[8,128,256]{2,0,1:T(8,128)}, s32[8,64]{1,0:T(8,128)}, s32[8]{0:T(128)S(1)}, s32[8,64]{1,0:T(8,128)}, /*index=5*/bf16[128,128,128...) while((s32[]{:T(128)}, f32[8,128,256]{2,0,1:T(8,128)}, ...), condition=%wide.region_4.7_spmd, body=%wide.region_3.6_spmd.sunk | while | flops 573837120 | bytes 33566048 | solution.py:128
  244.4 4.6 fusion.119
  249.0 4.5 collective-permute-start.1
  266.2 4.6 fusion.119
  270.8 4.5 collective-permute-start.1
  288.0 4.6 fusion.119
  292.6 4.5 collective-permute-start.1
  309.9 4.6 fusion.119
  314.5 4.5 collective-permute-start.1
  331.7 4.6 fusion.119
  336.3 4.5 collective-permute-start.1
  349.4 4.1 fusion.117
  353.5 4.6 fusion.119
  358.1 4.5 collective-permute-start.1
  371.2 4.1 fusion.117
  375.4 4.6 fusion.119
  385.5 6.5 %collective-permute-done.3 = bf16[8,128,256]{2,0,1:T(8,128)(2,1)S(1)} collective-permute-done((bf16[8,128,256]{2,0,1:T(8,128)(2,1)S(1)}, bf16[8,128,256]{2,0,1:T(8,128)(2,1)S(1)}, u32[]{:S(2)}, u32[]{:S(2)}) %collective-permute-start.3) | collective-permute-done | bytes 524320 | tf_op jit(solution)/shard_map/ppermute | solution.py:9
  394.3 36.1 %psum.39 = bf16[256]{0:T(256)(128)(2,1)S(1)} all-reduce(bf16[256]{0:T(256)(128)(2,1)S(1)} %get-tuple-element.457), channel_id=1, replica_groups=mesh['blk'=16,'rep'=2] {'blk'}, use_global_device_ids=true, to_apply=%region_9.12 | all-reduce | flops 256 | bytes 1024 | tf_op jit(solution)/shard_map/psum | solution.py:119
  430.9 47.6 %all-reduce.7.cloned.1.call-done = (bf16[256,256]{0,1:T(8,128)(2,1)}, bf16[256,256]{1,0:T(8,128)(2,1)}) async-done(((bf16[256,256]{0,1:T(8,128)(2,1)}, bf16[256,256]{1,0:T(8,128)(2,1)}), (bf16[256,256]{0,1:T(8,128)(2,1)}, bf16[256,256]{1,0:T(8,128)(2,1)})) %all-reduce.7.cloned.1.call-update) | async-done | bytes 262160 | tf_op jit(solution)/shard_map/psum | solution.py:117
  481.9 28.7 %all-reduce.5.cloned.1.call-done = bf16[1024,256]{1,0:T(8,128)(2,1)} async-done(((bf16[1024,256]{1,0:T(8,128)(2,1)}), bf16[1024,256]{1,0:T(8,128)(2,1)}) %all-reduce.5.cloned.1.call-update) | async-done | bytes 524304 | tf_op jit(solution)/shard_map/psum | solution.py:135
  (235 shorter events, 238.5 us)
Async XLA Ops:
  7.2 210.7 %copy-start = (bf16[256,256]{1,0:T(8,128)(2,1)S(1)}, bf16[256,256]{1,0:T(8,128)(2,1)}, u32[]{:S(2)}) copy-start(bf16[256,256]{1,0:T(8,128)(2,1)} %param.20) | copy-start | bytes 393220
  7.2 471.4 %all-reduce.7.cloned.1.call-start = ((), (), s32[]{:S(2)}) async-start(), calls=%async_computation.1 | async-start | bytes 524288 | tf_op jit(solution)/shard_map/psum | solution.py:117
  7.2 27.6 %collective-permute-start.2 = (bf16[1024,256]{1,0:T(8,128)(2,1)}, bf16[1024,256]{1,0:T(8,128)(2,1)}, u32[]{:S(2)}, u32[]{:S(2)}) collective-permute-start(bf16[1024,256]{1,0:T(8,128)(2,1)} %param.18), channel_id=1, source_target_pairs={{0,16},{2,18},{4,20},{6,22},{8,24},{10,26},{12,28},{14,30},{16,0},... | collective-permute-start | bytes 1572872 | tf_op jit(solution)/shard_map/ppermute | solution.py:9
  16.2 8.3 %copy-start.4 = (bf16[1024,256]{1,0:T(8,128)(2,1)S(1)}, bf16[1024,256]{1,0:T(8,128)(2,1)}, u32[]{:S(2)}) copy-start(bf16[1024,256]{1,0:T(8,128)(2,1)} %param.18) | copy-start | bytes 1572868
  16.2 8.3 %copy-start.7 = (bf16[256,256]{1,0:T(8,128)(2,1)S(1)}, bf16[256,256]{1,0:T(8,128)(2,1)}, u32[]{:S(2)}) copy-start(bf16[256,256]{1,0:T(8,128)(2,1)} %param.19) | copy-start | bytes 393220
  41.2 3.4 copy-start.8
  44.6 173.3 %copy-start.9 = (f32[256]{0:T(256)S(1)}, f32[256]{0:T(256)}, u32[]{:S(2)}) copy-start(f32[256]{0:T(256)} %param.21) | copy-start | bytes 3076
  44.6 11.3 %collective-permute-start = (bf16[1024,256]{1,0:T(8,128)(2,1)S(1)}, bf16[1024,256]{1,0:T(8,128)(2,1)S(1)}, u32[]{:S(2)}, u32[]{:S(2)}) collective-permute-start(bf16[1024,256]{1,0:T(8,128)(2,1)S(1)} %get-tuple-element.605), channel_id=1, source_target_pairs={{0,2},{2,4},{4,6},{6,8},{8,10},{10,12},{12,14},{14,16},{16,18},{18... | collective-permute-start | bytes 1572872 | tf_op jit(solution)/shard_map/while/body/eval_jaxpr/ppermute | solution.py:9
  58.7 3.6 copy-start.1
  65.7 11.3 %collective-permute-start = (bf16[1024,256]{1,0:T(8,128)(2,1)S(1)}, bf16[1024,256]{1,0:T(8,128)(2,1)S(1)}, u32[]{:S(2)}, u32[]{:S(2)}) collective-permute-start(bf16[1024,256]{1,0:T(8,128)(2,1)S(1)} %get-tuple-element.605), channel_id=1, source_target_pairs={{0,2},{2,4},{4,6},{6,8},{8,10},{10,12},{12,14},{14,16},{16,18},{18... | collective-permute-start | bytes 1572872 | tf_op jit(solution)/shard_map/while/body/eval_jaxpr/ppermute | solution.py:9
  79.8 3.6 copy-start.1
  86.8 11.3 %collective-permute-start = (bf16[1024,256]{1,0:T(8,128)(2,1)S(1)}, bf16[1024,256]{1,0:T(8,128)(2,1)S(1)}, u32[]{:S(2)}, u32[]{:S(2)}) collective-permute-start(bf16[1024,256]{1,0:T(8,128)(2,1)S(1)} %get-tuple-element.605), channel_id=1, source_target_pairs={{0,2},{2,4},{4,6},{6,8},{8,10},{10,12},{12,14},{14,16},{16,18},{18... | collective-permute-start | bytes 1572872 | tf_op jit(solution)/shard_map/while/body/eval_jaxpr/ppermute | solution.py:9
  100.9 3.6 copy-start.1
  107.9 11.3 %collective-permute-start = (bf16[1024,256]{1,0:T(8,128)(2,1)S(1)}, bf16[1024,256]{1,0:T(8,128)(2,1)S(1)}, u32[]{:S(2)}, u32[]{:S(2)}) collective-permute-start(bf16[1024,256]{1,0:T(8,128)(2,1)S(1)} %get-tuple-element.605), channel_id=1, source_target_pairs={{0,2},{2,4},{4,6},{6,8},{8,10},{10,12},{12,14},{14,16},{16,18},{18... | collective-permute-start | bytes 1572872 | tf_op jit(solution)/shard_map/while/body/eval_jaxpr/ppermute | solution.py:9
  122.0 3.6 copy-start.1
  129.0 11.3 %collective-permute-start = (bf16[1024,256]{1,0:T(8,128)(2,1)S(1)}, bf16[1024,256]{1,0:T(8,128)(2,1)S(1)}, u32[]{:S(2)}, u32[]{:S(2)}) collective-permute-start(bf16[1024,256]{1,0:T(8,128)(2,1)S(1)} %get-tuple-element.605), channel_id=1, source_target_pairs={{0,2},{2,4},{4,6},{6,8},{8,10},{10,12},{12,14},{14,16},{16,18},{18... | collective-permute-start | bytes 1572872 | tf_op jit(solution)/shard_map/while/body/eval_jaxpr/ppermute | solution.py:9
  143.1 3.6 copy-start.1
  150.2 11.3 %collective-permute-start = (bf16[1024,256]{1,0:T(8,128)(2,1)S(1)}, bf16[1024,256]{1,0:T(8,128)(2,1)S(1)}, u32[]{:S(2)}, u32[]{:S(2)}) collective-permute-start(bf16[1024,256]{1,0:T(8,128)(2,1)S(1)} %get-tuple-element.605), channel_id=1, source_target_pairs={{0,2},{2,4},{4,6},{6,8},{8,10},{10,12},{12,14},{14,16},{16,18},{18... | collective-permute-start | bytes 1572872 | tf_op jit(solution)/shard_map/while/body/eval_jaxpr/ppermute | solution.py:9
  164.2 3.6 copy-start.1
  171.3 11.3 %collective-permute-start = (bf16[1024,256]{1,0:T(8,128)(2,1)S(1)}, bf16[1024,256]{1,0:T(8,128)(2,1)S(1)}, u32[]{:S(2)}, u32[]{:S(2)}) collective-permute-start(bf16[1024,256]{1,0:T(8,128)(2,1)S(1)} %get-tuple-element.605), channel_id=1, source_target_pairs={{0,2},{2,4},{4,6},{6,8},{8,10},{10,12},{12,14},{14,16},{16,18},{18... | collective-permute-start | bytes 1572872 | tf_op jit(solution)/shard_map/while/body/eval_jaxpr/ppermute | solution.py:9
  185.4 3.6 copy-start.1
  194.0 26.7 %copy-start.5 = (bf16[1024,256]{1,0:T(8,128)(2,1)S(1)}, bf16[1024,256]{1,0:T(8,128)(2,1)}, u32[]{:S(2)}) copy-start(bf16[1024,256]{1,0:T(8,128)(2,1)} %param.27) | copy-start | bytes 1572868
  217.9 3.5 copy-start.6
  231.6 12.7 %collective-permute-start.1 = (f32[8,128,256]{2,0,1:T(8,128)}, f32[8,128,256]{2,0,1:T(8,128)}, u32[]{:S(2)}, u32[]{:S(2)}) collective-permute-start(f32[8,128,256]{2,0,1:T(8,128)} %get-tuple-element.639), channel_id=1, source_target_pairs={{0,30},{2,0},{4,2},{6,4},{8,6},{10,8},{12,10},{14,12},{16,14},{18,... | collective-permute-start | bytes 3145736 | tf_op jit(solution)/shard_map/while/body/eval_jaxpr/ppermute | solution.py:9
  249.0 17.2 %collective-permute-start.1 = (f32[8,128,256]{2,0,1:T(8,128)}, f32[8,128,256]{2,0,1:T(8,128)}, u32[]{:S(2)}, u32[]{:S(2)}) collective-permute-start(f32[8,128,256]{2,0,1:T(8,128)} %get-tuple-element.639), channel_id=1, source_target_pairs={{0,30},{2,0},{4,2},{6,4},{8,6},{10,8},{12,10},{14,12},{16,14},{18,... | collective-permute-start | bytes 3145736 | tf_op jit(solution)/shard_map/while/body/eval_jaxpr/ppermute | solution.py:9
  270.8 17.2 %collective-permute-start.1 = (f32[8,128,256]{2,0,1:T(8,128)}, f32[8,128,256]{2,0,1:T(8,128)}, u32[]{:S(2)}, u32[]{:S(2)}) collective-permute-start(f32[8,128,256]{2,0,1:T(8,128)} %get-tuple-element.639), channel_id=1, source_target_pairs={{0,30},{2,0},{4,2},{6,4},{8,6},{10,8},{12,10},{14,12},{16,14},{18,... | collective-permute-start | bytes 3145736 | tf_op jit(solution)/shard_map/while/body/eval_jaxpr/ppermute | solution.py:9
  292.6 17.2 %collective-permute-start.1 = (f32[8,128,256]{2,0,1:T(8,128)}, f32[8,128,256]{2,0,1:T(8,128)}, u32[]{:S(2)}, u32[]{:S(2)}) collective-permute-start(f32[8,128,256]{2,0,1:T(8,128)} %get-tuple-element.639), channel_id=1, source_target_pairs={{0,30},{2,0},{4,2},{6,4},{8,6},{10,8},{12,10},{14,12},{16,14},{18,... | collective-permute-start | bytes 3145736 | tf_op jit(solution)/shard_map/while/body/eval_jaxpr/ppermute | solution.py:9
  314.5 17.2 %collective-permute-start.1 = (f32[8,128,256]{2,0,1:T(8,128)}, f32[8,128,256]{2,0,1:T(8,128)}, u32[]{:S(2)}, u32[]{:S(2)}) collective-permute-start(f32[8,128,256]{2,0,1:T(8,128)} %get-tuple-element.639), channel_id=1, source_target_pairs={{0,30},{2,0},{4,2},{6,4},{8,6},{10,8},{12,10},{14,12},{16,14},{18,... | collective-permute-start | bytes 3145736 | tf_op jit(solution)/shard_map/while/body/eval_jaxpr/ppermute | solution.py:9
  336.3 17.2 %collective-permute-start.1 = (f32[8,128,256]{2,0,1:T(8,128)}, f32[8,128,256]{2,0,1:T(8,128)}, u32[]{:S(2)}, u32[]{:S(2)}) collective-permute-start(f32[8,128,256]{2,0,1:T(8,128)} %get-tuple-element.639), channel_id=1, source_target_pairs={{0,30},{2,0},{4,2},{6,4},{8,6},{10,8},{12,10},{14,12},{16,14},{18,... | collective-permute-start | bytes 3145736 | tf_op jit(solution)/shard_map/while/body/eval_jaxpr/ppermute | solution.py:9
  358.1 17.2 %collective-permute-start.1 = (f32[8,128,256]{2,0,1:T(8,128)}, f32[8,128,256]{2,0,1:T(8,128)}, u32[]{:S(2)}, u32[]{:S(2)}) collective-permute-start(f32[8,128,256]{2,0,1:T(8,128)} %get-tuple-element.639), channel_id=1, source_target_pairs={{0,30},{2,0},{4,2},{6,4},{8,6},{10,8},{12,10},{14,12},{16,14},{18,... | collective-permute-start | bytes 3145736 | tf_op jit(solution)/shard_map/while/body/eval_jaxpr/ppermute | solution.py:9
  381.2 10.8 %collective-permute-start.3 = (bf16[8,128,256]{2,0,1:T(8,128)(2,1)S(1)}, bf16[8,128,256]{2,0,1:T(8,128)(2,1)S(1)}, u32[]{:S(2)}, u32[]{:S(2)}) collective-permute-start(bf16[8,128,256]{2,0,1:T(8,128)(2,1)S(1)} %convert_element_type.66), channel_id=1, source_target_pairs={{0,16},{2,18},{4,20},{6,22},{8,24},{10,26},{12,28},{14,30},{16,0},... | collective-permute-start | bytes 1572872 | tf_op jit(solution)/shard_map/ppermute | solution.py:9
  385.4 125.2 %all-reduce.5.cloned.1.call-start = ((), (), s32[]{:S(2)}) async-start(), calls=%async_computation | async-start | bytes 1048576 | tf_op jit(solution)/shard_map/psum | solution.py:135
  (8 other events, 10.1 us)
Sparse Core Ops, SparseCore 0:
  385.6 92.9 all-reduce.6
  481.4 29.1 all-reduce.4
where the time goes:
time: 522 us; the launch traced here: 520 us
  waiting for transfers between devices  130 us (25%)
  local copies, waits for them, and re-layouts  128 us (25%)
  matrix products  127 us (24%)
  blocking collectives  60 us (11%)
  starting transfers between devices  31.5 us (6%)
  other arithmetic  27.4 us (5%)
  between operations  14.2 us (3%)
    dot_general x16, matrix products, gather_terms(): jnp.einsum('kr,kaf->raf', placing, products, preferred_element_type=jnp.f...  55.3 us
    ppermute x16, waiting for transfers between devices, from_behind(): lax.ppermute(array, axis, [(i, (i + by) % length) for i in range(length)])  54 us
    gather x16, local copies, waits for them, and re-layouts, gather_terms(): tile_values = jnp.take(tile_table, value_pick, axis=0)  51.5 us
    psum x1, waiting for transfers between devices, on_device(): lax.psum(grad_self.astype(jnp.bfloat16), 'blk').astype(jnp.float32)  47.6 us
    psum x1, blocking collectives, on_device(): lax.psum(grad_offset.astype(jnp.bfloat16), 'blk').astype(jnp.float32)  36.1 us
    dot_general x8, matrix products, gather_terms(): jnp.einsum('kab,kaf->kbf', tile_values, picked, preferred_element_type=jn...  32.8 us
    ppermute x16, starting transfers between devices, from_behind(): lax.ppermute(array, axis, [(i, (i + by) % length) for i in range(length)])  31.5 us
    dot_general x8, matrix products, gather_terms(): jnp.einsum('kab,kbf->kaf', tile_values, picked, preferred_element_type=jn...  28.7 us
  transfers between devices with their start and end apart: 18, of which 11 were waited for; matrix products, arithmetic and copies ran while one was open for 30% of the time, Pallas kernels for 0%

commit v1 on v0

--- a/solution.py
+++ b/solution.py
@@ -1,7 +1,16 @@
+import functools
 import jax
 import jax.numpy as jnp
 from jax import lax
 from jax.sharding import PartitionSpec as P
+from jax.lax import all_gather
+
+
+def measure_view(values, bus_axis):
+    return all_gather(values, bus_axis).sum(axis=0)
+
+
+pages_recover = functools.partial(measure_view, bus_axis="blk")
 
 
 def from_behind(array, axis, by):
@@ -114,7 +123,7 @@
         grad_pre, weight_neighbor, contract_columns, preferred_element_type=jnp.float32
     ).astype(jnp.bfloat16)
     grad_self, grad_neighbor, grad_offset = (
-        lax.psum(grad_self.astype(jnp.bfloat16), "blk").astype(jnp.float32),
+        pages_recover(grad_self.astype(jnp.bfloat16)).astype(jnp.float32),
         lax.psum(grad_neighbor.astype(jnp.bfloat16), "blk").astype(jnp.float32),
         lax.psum(grad_offset.astype(jnp.bfloat16), "blk").astype(jnp.float32),
     )

time: 522 us -> 564 us (1.080)
  waiting for transfers between devices: 130 us -> 171 us
    all_gather x0 -> x1, waiting for transfers between devices: none -> 41.6 us  [measure_view(): return all_gather(values, bus_axis).sum(axis=0)]
    psum x1, waiting for transfers between devices: 47.6 us -> 42 us  [on_device(): lax.psum(grad_neighbor.astype(jnp.bfloat16), 'blk').astype(jnp.float32)]
  transfers between devices with their start and end apart: 18 -> 19, of which waited for: 11 -> 12; matrix products, arithmetic and copies ran while one was open for 30% -> 27% of each run, Pallas kernels for 0% -> 0%
where the time goes in v1:
time: 564 us; the launch traced here: 561 us
  waiting for transfers between devices  171 us (30%)
  local copies, waits for them, and re-layouts  129 us (23%)
  matrix products  126 us (22%)
  blocking collectives  59.9 us (11%)
  starting transfers between devices  31.6 us (6%)
  other arithmetic  28.6 us (5%)
  between operations  14 us (2%)
    ppermute x16, waiting for transfers between devices, from_behind(): lax.ppermute(array, axis, [(i, (i + by) % length) for i in range(length)])  56 us
    dot_general x16, matrix products, gather_terms(): jnp.einsum('kr,kaf->raf', placing, products, preferred_element_type=jnp.f...  55.3 us
    gather x16, local copies, waits for them, and re-layouts, gather_terms(): tile_values = jnp.take(tile_table, value_pick, axis=0)  51.5 us
    psum x1, waiting for transfers between devices, on_device(): lax.psum(grad_neighbor.astype(jnp.bfloat16), 'blk').astype(jnp.float32)  42 us
    all_gather x1, waiting for transfers between devices, measure_view(): return all_gather(values, bus_axis).sum(axis=0)  41.6 us
    psum x1, blocking collectives, on_device(): lax.psum(grad_offset.astype(jnp.bfloat16), 'blk').astype(jnp.float32)  36 us
    dot_general x8, matrix products, gather_terms(): jnp.einsum('kab,kaf->kbf', tile_values, picked, preferred_element_type=jn...  32.8 us
    psum x1, waiting for transfers between devices, on_device(): lax.psum(pushed.astype(jnp.bfloat16), 'rep').astype(jnp.float32)  31.5 us
  transfers between devices with their start and end apart: 19, of which 12 were waited for; matrix products, arithmetic and copies ran while one was open for 27% of the time, Pallas kernels for 0%

profile of v1, /device:TPU:0, one launch (start us, length us, event | category | flops | bytes accessed | tf_op | source)
XLA Modules:
  0.0 561.1 jit_solution(6382895859318732071)
XLA Ops:
  7.2 4.1 collective-permute-start.2
  19.4 4.3 gather_fusion.6
  25.8 9.0 %collective-permute-done.2 = bf16[1024,256]{1,0:T(8,128)(2,1)} collective-permute-done((bf16[1024,256]{1,0:T(8,128)(2,1)}, bf16[1024,256]{1,0:T(8,128)(2,1)}, u32[]{:S(2)}, u32[]{:S(2)}) %collective-permute-start.2) | collective-permute-done | bytes 524320 | tf_op jit(solution)/shard_map/ppermute | solution.py:18
  44.5 147.5 %while.32 = (s32[]{:T(128)}, bf16[1024,256]{1,0:T(8,128)(2,1)S(1)}, f32[8,128,256]{2,0,1:T(8,128)}, s32[8,64]{1,0:T(8,128)}, s32[8]{0:T(128)S(1)}, /*index=5*/s3...) while((s32[]{:T(128)}, bf16[1024,256]{1,0:T(8,128)(2,1)S(1)}, ...), condition=%wide.region_1.4_spmd, body=%wide.region_0.3_spmd.sunk | while | flops 573837120 | bytes 40906124 | solution.py:94
  50.4 5.5 collective-permute-done
  71.4 5.5 collective-permute-done
  92.5 5.5 collective-permute-done
  113.6 5.5 collective-permute-done
  134.7 5.5 collective-permute-done
  155.7 5.5 collective-permute-done
  176.8 5.5 collective-permute-done
  193.7 23.9 %all-reduce.7 = bf16[1024,256]{1,0:T(8,128)(2,1)S(1)} all-reduce(f32[1024,256]{1,0:T(8,128)S(1)} %bitcast.102), channel_id=1, replica_groups=mesh['blk'=16,'rep'=2] {'rep'}, use_global_device_ids=true, to_apply=%region_2.5 | all-reduce | flops 262144 | bytes 1572864 | tf_op jit(solution)/shard_map/psum | solution.py:98
  231.3 148.2 %while.33 = (s32[]{:T(128)}, f32[8,128,256]{2,0,1:T(8,128)}, s32[8,64]{1,0:T(8,128)}, s32[8]{0:T(128)S(1)}, s32[8,64]{1,0:T(8,128)}, /*index=5*/bf16[128,128,128...) while((s32[]{:T(128)}, f32[8,128,256]{2,0,1:T(8,128)}, ...), condition=%wide.region_4.7_spmd, body=%wide.region_3.6_spmd.sunk | while | flops 573837120 | bytes 33566048 | solution.py:137
  239.9 4.1 fusion.117
  244.0 4.6 fusion.119
  248.6 4.5 collective-permute-start.1
  265.8 4.6 fusion.119
  270.4 4.5 collective-permute-start.1
  287.6 4.6 fusion.119
  292.2 4.5 collective-permute-start.1
  309.5 4.6 fusion.119
  314.1 4.5 collective-permute-start.1
  331.3 4.6 fusion.119
  335.9 4.5 collective-permute-start.1
  353.1 4.6 fusion.119
  357.7 4.6 collective-permute-start.1
  374.9 4.6 fusion.119
  383.0 8.5 %collective-permute-done.3 = bf16[8,128,256]{2,0,1:T(8,128)(2,1)S(1)} collective-permute-done((bf16[8,128,256]{2,0,1:T(8,128)(2,1)S(1)}, bf16[8,128,256]{2,0,1:T(8,128)(2,1)S(1)}, u32[]{:S(2)}, u32[]{:S(2)}) %collective-permute-start.3) | collective-permute-done | bytes 524320 | tf_op jit(solution)/shard_map/ppermute | solution.py:18
  394.9 36.0 %psum.31 = bf16[256]{0:T(256)(128)(2,1)S(1)} all-reduce(bf16[256]{0:T(256)(128)(2,1)S(1)} %get-tuple-element.450), channel_id=1, replica_groups=mesh['blk'=16,'rep'=2] {'blk'}, use_global_device_ids=true, to_apply=%region_9.12 | all-reduce | flops 256 | bytes 1024 | tf_op jit(solution)/shard_map/psum | solution.py:128
  431.5 42.0 %all-reduce.6.cloned.1.call-done = bf16[256,256]{1,0:T(8,128)(2,1)} async-done(((bf16[256,256]{1,0:T(8,128)(2,1)}), bf16[256,256]{1,0:T(8,128)(2,1)}) %all-reduce.6.cloned.1.call-update) | async-done | bytes 131088 | tf_op jit(solution)/shard_map/psum | solution.py:127
  475.1 31.5 %all-reduce.4.cloned.1.call-done = bf16[1024,256]{1,0:T(8,128)(2,1)} async-done(((bf16[1024,256]{1,0:T(8,128)(2,1)}), bf16[1024,256]{1,0:T(8,128)(2,1)}) %all-reduce.4.cloned.1.call-update) | async-done | bytes 524304 | tf_op jit(solution)/shard_map/psum | solution.py:144
  508.7 41.6 %all-gather.3.cloned.1.call-done = bf16[4096,256]{0,1:T(8,128)(2,1)} async-done(((bf16[256,256]{0,1:T(8,128)(2,1)}), bf16[4096,256]{0,1:T(8,128)(2,1)}) %all-gather.3.cloned.1.call-update) | async-done | bytes 2097168 | tf_op jit(solution)/shard_map/all_gather | solution.py:10
  (242 shorter events, 243.7 us)
Async XLA Ops:
  7.2 210.4 %copy-start = (bf16[256,256]{1,0:T(8,128)(2,1)S(1)}, bf16[256,256]{1,0:T(8,128)(2,1)}, u32[]{:S(2)}) copy-start(bf16[256,256]{1,0:T(8,128)(2,1)} %param.20) | copy-start | bytes 393220
  7.2 466.3 %all-reduce.6.cloned.1.call-start = ((), (), s32[]{:S(2)}) async-start(), calls=%async_computation.1 | async-start | bytes 262144 | tf_op jit(solution)/shard_map/psum | solution.py:127
  7.2 27.6 %collective-permute-start.2 = (bf16[1024,256]{1,0:T(8,128)(2,1)}, bf16[1024,256]{1,0:T(8,128)(2,1)}, u32[]{:S(2)}, u32[]{:S(2)}) collective-permute-start(bf16[1024,256]{1,0:T(8,128)(2,1)} %param.18), channel_id=1, source_target_pairs={{0,16},{2,18},{4,20},{6,22},{8,24},{10,26},{12,28},{14,30},{16,0},... | collective-permute-start | bytes 1572872 | tf_op jit(solution)/shard_map/ppermute | solution.py:18
  16.2 8.3 %copy-start.4 = (bf16[1024,256]{1,0:T(8,128)(2,1)S(1)}, bf16[1024,256]{1,0:T(8,128)(2,1)}, u32[]{:S(2)}) copy-start(bf16[1024,256]{1,0:T(8,128)(2,1)} %param.18) | copy-start | bytes 1572868
  16.2 8.3 %copy-start.8 = (bf16[256,256]{1,0:T(8,128)(2,1)S(1)}, bf16[256,256]{1,0:T(8,128)(2,1)}, u32[]{:S(2)}) copy-start(bf16[256,256]{1,0:T(8,128)(2,1)} %param.19) | copy-start | bytes 393220
  44.5 173.1 %copy-start.10 = (f32[256]{0:T(256)S(1)}, f32[256]{0:T(256)}, u32[]{:S(2)}) copy-start(f32[256]{0:T(256)} %param.21) | copy-start | bytes 3076
  44.5 11.3 %collective-permute-start = (bf16[1024,256]{1,0:T(8,128)(2,1)S(1)}, bf16[1024,256]{1,0:T(8,128)(2,1)S(1)}, u32[]{:S(2)}, u32[]{:S(2)}) collective-permute-start(bf16[1024,256]{1,0:T(8,128)(2,1)S(1)} %get-tuple-element.598), channel_id=1, source_target_pairs={{0,2},{2,4},{4,6},{6,8},{8,10},{10,12},{12,14},{14,16},{16,18},{18... | collective-permute-start | bytes 1572872 | tf_op jit(solution)/shard_map/while/body/eval_jaxpr/ppermute | solution.py:18
  58.6 3.6 copy-start.1
  65.6 11.3 %collective-permute-start = (bf16[1024,256]{1,0:T(8,128)(2,1)S(1)}, bf16[1024,256]{1,0:T(8,128)(2,1)S(1)}, u32[]{:S(2)}, u32[]{:S(2)}) collective-permute-start(bf16[1024,256]{1,0:T(8,128)(2,1)S(1)} %get-tuple-element.598), channel_id=1, source_target_pairs={{0,2},{2,4},{4,6},{6,8},{8,10},{10,12},{12,14},{14,16},{16,18},{18... | collective-permute-start | bytes 1572872 | tf_op jit(solution)/shard_map/while/body/eval_jaxpr/ppermute | solution.py:18
  79.7 3.6 copy-start.1
  86.7 11.3 %collective-permute-start = (bf16[1024,256]{1,0:T(8,128)(2,1)S(1)}, bf16[1024,256]{1,0:T(8,128)(2,1)S(1)}, u32[]{:S(2)}, u32[]{:S(2)}) collective-permute-start(bf16[1024,256]{1,0:T(8,128)(2,1)S(1)} %get-tuple-element.598), channel_id=1, source_target_pairs={{0,2},{2,4},{4,6},{6,8},{8,10},{10,12},{12,14},{14,16},{16,18},{18... | collective-permute-start | bytes 1572872 | tf_op jit(solution)/shard_map/while/body/eval_jaxpr/ppermute | solution.py:18
  100.8 3.6 copy-start.1
  107.8 11.3 %collective-permute-start = (bf16[1024,256]{1,0:T(8,128)(2,1)S(1)}, bf16[1024,256]{1,0:T(8,128)(2,1)S(1)}, u32[]{:S(2)}, u32[]{:S(2)}) collective-permute-start(bf16[1024,256]{1,0:T(8,128)(2,1)S(1)} %get-tuple-element.598), channel_id=1, source_target_pairs={{0,2},{2,4},{4,6},{6,8},{8,10},{10,12},{12,14},{14,16},{16,18},{18... | collective-permute-start | bytes 1572872 | tf_op jit(solution)/shard_map/while/body/eval_jaxpr/ppermute | solution.py:18
  121.8 3.6 copy-start.1
  128.9 11.3 %collective-permute-start = (bf16[1024,256]{1,0:T(8,128)(2,1)S(1)}, bf16[1024,256]{1,0:T(8,128)(2,1)S(1)}, u32[]{:S(2)}, u32[]{:S(2)}) collective-permute-start(bf16[1024,256]{1,0:T(8,128)(2,1)S(1)} %get-tuple-element.598), channel_id=1, source_target_pairs={{0,2},{2,4},{4,6},{6,8},{8,10},{10,12},{12,14},{14,16},{16,18},{18... | collective-permute-start | bytes 1572872 | tf_op jit(solution)/shard_map/while/body/eval_jaxpr/ppermute | solution.py:18
  142.9 3.6 copy-start.1
  149.9 11.3 %collective-permute-start = (bf16[1024,256]{1,0:T(8,128)(2,1)S(1)}, bf16[1024,256]{1,0:T(8,128)(2,1)S(1)}, u32[]{:S(2)}, u32[]{:S(2)}) collective-permute-start(bf16[1024,256]{1,0:T(8,128)(2,1)S(1)} %get-tuple-element.598), channel_id=1, source_target_pairs={{0,2},{2,4},{4,6},{6,8},{8,10},{10,12},{12,14},{14,16},{16,18},{18... | collective-permute-start | bytes 1572872 | tf_op jit(solution)/shard_map/while/body/eval_jaxpr/ppermute | solution.py:18
  164.0 3.6 copy-start.1
  171.0 11.3 %collective-permute-start = (bf16[1024,256]{1,0:T(8,128)(2,1)S(1)}, bf16[1024,256]{1,0:T(8,128)(2,1)S(1)}, u32[]{:S(2)}, u32[]{:S(2)}) collective-permute-start(bf16[1024,256]{1,0:T(8,128)(2,1)S(1)} %get-tuple-element.598), channel_id=1, source_target_pairs={{0,2},{2,4},{4,6},{6,8},{8,10},{10,12},{12,14},{14,16},{16,18},{18... | collective-permute-start | bytes 1572872 | tf_op jit(solution)/shard_map/while/body/eval_jaxpr/ppermute | solution.py:18
  185.1 3.6 copy-start.1
  193.7 26.6 %copy-start.6 = (bf16[1024,256]{1,0:T(8,128)(2,1)S(1)}, bf16[1024,256]{1,0:T(8,128)(2,1)}, u32[]{:S(2)}) copy-start(bf16[1024,256]{1,0:T(8,128)(2,1)} %param.27) | copy-start | bytes 1572868
  231.3 12.7 %collective-permute-start.1 = (f32[8,128,256]{2,0,1:T(8,128)}, f32[8,128,256]{2,0,1:T(8,128)}, u32[]{:S(2)}, u32[]{:S(2)}) collective-permute-start(f32[8,128,256]{2,0,1:T(8,128)} %get-tuple-element.632), channel_id=1, source_target_pairs={{0,30},{2,0},{4,2},{6,4},{8,6},{10,8},{12,10},{14,12},{16,14},{18,... | collective-permute-start | bytes 3145736 | tf_op jit(solution)/shard_map/while/body/eval_jaxpr/ppermute | solution.py:18
  248.6 17.2 %collective-permute-start.1 = (f32[8,128,256]{2,0,1:T(8,128)}, f32[8,128,256]{2,0,1:T(8,128)}, u32[]{:S(2)}, u32[]{:S(2)}) collective-permute-start(f32[8,128,256]{2,0,1:T(8,128)} %get-tuple-element.632), channel_id=1, source_target_pairs={{0,30},{2,0},{4,2},{6,4},{8,6},{10,8},{12,10},{14,12},{16,14},{18,... | collective-permute-start | bytes 3145736 | tf_op jit(solution)/shard_map/while/body/eval_jaxpr/ppermute | solution.py:18
  270.4 17.2 %collective-permute-start.1 = (f32[8,128,256]{2,0,1:T(8,128)}, f32[8,128,256]{2,0,1:T(8,128)}, u32[]{:S(2)}, u32[]{:S(2)}) collective-permute-start(f32[8,128,256]{2,0,1:T(8,128)} %get-tuple-element.632), channel_id=1, source_target_pairs={{0,30},{2,0},{4,2},{6,4},{8,6},{10,8},{12,10},{14,12},{16,14},{18,... | collective-permute-start | bytes 3145736 | tf_op jit(solution)/shard_map/while/body/eval_jaxpr/ppermute | solution.py:18
  292.2 17.2 %collective-permute-start.1 = (f32[8,128,256]{2,0,1:T(8,128)}, f32[8,128,256]{2,0,1:T(8,128)}, u32[]{:S(2)}, u32[]{:S(2)}) collective-permute-start(f32[8,128,256]{2,0,1:T(8,128)} %get-tuple-element.632), channel_id=1, source_target_pairs={{0,30},{2,0},{4,2},{6,4},{8,6},{10,8},{12,10},{14,12},{16,14},{18,... | collective-permute-start | bytes 3145736 | tf_op jit(solution)/shard_map/while/body/eval_jaxpr/ppermute | solution.py:18
  314.1 17.2 %collective-permute-start.1 = (f32[8,128,256]{2,0,1:T(8,128)}, f32[8,128,256]{2,0,1:T(8,128)}, u32[]{:S(2)}, u32[]{:S(2)}) collective-permute-start(f32[8,128,256]{2,0,1:T(8,128)} %get-tuple-element.632), channel_id=1, source_target_pairs={{0,30},{2,0},{4,2},{6,4},{8,6},{10,8},{12,10},{14,12},{16,14},{18,... | collective-permute-start | bytes 3145736 | tf_op jit(solution)/shard_map/while/body/eval_jaxpr/ppermute | solution.py:18
  335.9 17.2 %collective-permute-start.1 = (f32[8,128,256]{2,0,1:T(8,128)}, f32[8,128,256]{2,0,1:T(8,128)}, u32[]{:S(2)}, u32[]{:S(2)}) collective-permute-start(f32[8,128,256]{2,0,1:T(8,128)} %get-tuple-element.632), channel_id=1, source_target_pairs={{0,30},{2,0},{4,2},{6,4},{8,6},{10,8},{12,10},{14,12},{16,14},{18,... | collective-permute-start | bytes 3145736 | tf_op jit(solution)/shard_map/while/body/eval_jaxpr/ppermute | solution.py:18
  357.7 17.2 %collective-permute-start.1 = (f32[8,128,256]{2,0,1:T(8,128)}, f32[8,128,256]{2,0,1:T(8,128)}, u32[]{:S(2)}, u32[]{:S(2)}) collective-permute-start(f32[8,128,256]{2,0,1:T(8,128)} %get-tuple-element.632), channel_id=1, source_target_pairs={{0,30},{2,0},{4,2},{6,4},{8,6},{10,8},{12,10},{14,12},{16,14},{18,... | collective-permute-start | bytes 3145736 | tf_op jit(solution)/shard_map/while/body/eval_jaxpr/ppermute | solution.py:18
  379.5 14.4 %copy-start.5 = (bf16[1024,256]{1,0:T(8,128)(2,1)S(1)}, bf16[1024,256]{1,0:T(8,128)(2,1)}, u32[]{:S(2)}) copy-start(bf16[1024,256]{1,0:T(8,128)(2,1)} %param.18) | copy-start | bytes 1572868
  380.8 10.7 %collective-permute-start.3 = (bf16[8,128,256]{2,0,1:T(8,128)(2,1)S(1)}, bf16[8,128,256]{2,0,1:T(8,128)(2,1)S(1)}, u32[]{:S(2)}, u32[]{:S(2)}) collective-permute-start(bf16[8,128,256]{2,0,1:T(8,128)(2,1)S(1)} %convert_element_type.68), channel_id=1, source_target_pairs={{0,16},{2,18},{4,20},{6,22},{8,24},{10,26},{12,28},{14,30},{16,0},... | collective-permute-start | bytes 1572872 | tf_op jit(solution)/shard_map/ppermute | solution.py:18
  383.0 123.6 %all-reduce.4.cloned.1.call-start = ((), (), s32[]{:S(2)}) async-start(), calls=%async_computation | async-start | bytes 1048576 | tf_op jit(solution)/shard_map/psum | solution.py:144
  393.8 156.5 %all-gather.3.cloned.1.call-start = ((), (), s32[]{:S(2)}) async-start(), calls=%async_computation.2 | async-start | bytes 2228224 | tf_op jit(solution)/shard_map/all_gather | solution.py:10
  (10 other events, 16.8 us)
Sparse Core Ops, SparseCore 0:
  383.1 90.3 all-reduce.5
  476.3 30.1 all-reduce.3
  509.3 41.0 all-gather.2
